TPU v7x, 32 devices: a whole 2x2x4 slice. The times are simulated.
32 devices in a mesh: groups: 2 (over y), tiles: 16 (over z, x, core).
Axes of the slice: x: 2, y: 2, z: 4, core: 2. Of those that a mesh axis runs over, the one named last changes fastest.
Arguments:
- raw: bfloat16 [16, 256, 2048], P(None, ('groups', 'tiles')), parts along dimension 1, may hold values from -40 to 40, as said below
- fir: float32 [64], replicated, may hold values from -0.75 to 0.75
- keep: int32 [16, 256], P(None, ('groups', 'tiles')), parts along dimension 1, may hold values 0 or 1
- table: int32 [16, 2], replicated, may hold values from 0 to 0, as said below
Outputs:
- stacks: bfloat16 [32, 128, 128, 256], P(('groups', 'tiles')), parts along dimension 0
There are 2 independent parts, one for each index of `groups`. A program takes and returns all parts, laid end to end along the dimension named above; an argument that names none is the same for every part. Nothing has to cross between parts.
Inputs may be any that keep to these rules, and one draw needn't show every extreme that they name: `table`: each row holds r <= c. `raw`: a common motion of all channels plus independent noise.
All inputs are finite; a program needn't handle non-finite values. No bound on the sum of `keep` on one device may be relied on, other than what follows from the above.
Results may differ from a plain program's by a relative error of at most 0.0053.
Values may be sent and summed in bfloat16 or wider, within the bound.
A program may use at most 128 MiB of HBM per device.

v0:
```python
import jax
import jax.numpy as jnp
from jax import lax
from jax.sharding import PartitionSpec as P

WINDOWS = 16
TILE = 128
SEG = 512
LAGS = 256
TAPS = 64
DEC = 4
RAW = 2048
NBIN = 256


def filter_band(fir):
    period = 2 * RAW + TAPS
    pattern = jnp.concatenate([fir[:1], jnp.zeros((period - TAPS,), jnp.float32), fir[1:][::-1]])
    tiled = jnp.tile(pattern, SEG)[: SEG * (period - DEC)].reshape(SEG, period - DEC)
    return tiled[:, :RAW]


def filter_block(raw, fir):
    band = filter_band(fir)
    return jnp.einsum("wcm,nm->wcn", raw.astype(jnp.float32), band, precision=lax.Precision.HIGHEST)


def dft_tables():
    steps = jnp.arange(SEG, dtype=jnp.int32)
    freqs = jnp.arange(NBIN, dtype=jnp.int32)
    angle = 2.0 * jnp.pi / SEG * jnp.mod(steps[:, None] * freqs[None, :], SEG).astype(jnp.float32)
    return (jnp.cos(angle), jnp.sin(angle))


def whiten(decimated, keep):
    cosine, sine = dft_tables()
    real_part = jnp.einsum("wcn,nf->wcf", decimated, cosine, precision=lax.Precision.HIGHEST)
    imag_part = -jnp.einsum("wcn,nf->wcf", decimated, sine, precision=lax.Precision.HIGHEST)
    power = real_part * real_part + imag_part * imag_part
    level = jnp.mean(power, -1, keepdims=True)
    scale = keep.astype(jnp.float32)[..., None] / jnp.sqrt(0.5 * power + 0.5 * level + 1e-05)
    return jnp.concatenate([real_part * scale, imag_part * scale], -1).astype(jnp.bfloat16)


def cross_tile(rows, cols):
    half = rows.shape[-1] // 2
    row_re, row_im = (rows[..., :half], rows[..., half:])
    col_re, col_im = (cols[..., :half], cols[..., half:])
    cross_re = jnp.einsum("wif,wjf->ijf", row_re, col_re, preferred_element_type=jnp.float32)
    cross_re = cross_re + jnp.einsum(
        "wif,wjf->ijf", row_im, col_im, preferred_element_type=jnp.float32
    )
    cross_im = jnp.einsum("wif,wjf->ijf", row_re, col_im, preferred_element_type=jnp.float32)
    cross_im = cross_im - jnp.einsum(
        "wif,wjf->ijf", row_im, col_re, preferred_element_type=jnp.float32
    )
    return jnp.concatenate([cross_re, cross_im], -1).astype(jnp.bfloat16)


def lag_rows(freqs, imaginary):
    shifts = jnp.arange(LAGS, dtype=jnp.int32) - LAGS // 2
    angle = 2.0 * jnp.pi / SEG * jnp.mod(freqs[:, None] * shifts[None, :], SEG).astype(jnp.float32)
    weight = jnp.where(freqs == 0, 1.0, 2.0).astype(jnp.float32)[:, None] / jnp.sqrt(
        jnp.float32(WINDOWS * NBIN)
    )
    return jnp.where(imaginary[:, None], -weight * jnp.sin(angle), weight * jnp.cos(angle)).astype(
        jnp.bfloat16
    )


def local(raw, fir, keep, table):
    devices = lax.axis_size("tiles")
    filtered = filter_block(raw, fir)
    channel_sum = lax.psum(jnp.sum(filtered, 1), "tiles")
    common = channel_sum[:, None, :] / (raw.shape[1] * devices)
    whitened = whiten(filtered - common, keep)
    entry = table[lax.axis_index("tiles")]
    row_base = entry[0] * TILE
    col_base = entry[1] * TILE
    offsets = jnp.arange(TILE, dtype=jnp.int32)
    piece = lax.all_gather(whitened, "tiles", axis=1, tiled=True)
    places = jnp.arange(piece.shape[1], dtype=jnp.int32)
    pick_rows = (places[None, :] == row_base + offsets[:, None]).astype(jnp.bfloat16)
    pick_cols = (places[None, :] == col_base + offsets[:, None]).astype(jnp.bfloat16)
    add_rows = jnp.einsum("in,wnf->wif", pick_rows, piece, preferred_element_type=jnp.float32)
    add_cols = jnp.einsum("in,wnf->wif", pick_cols, piece, preferred_element_type=jnp.float32)
    rows = add_rows.astype(jnp.bfloat16)
    cols = add_cols.astype(jnp.bfloat16)
    cross = cross_tile(rows, cols).reshape(TILE * TILE, 2 * NBIN)
    freqs = jnp.concatenate([jnp.arange(NBIN, dtype=jnp.int32)] * 2)
    imaginary = jnp.arange(2 * NBIN, dtype=jnp.int32) >= NBIN
    lags = lag_rows(freqs, imaginary)
    stacked = jnp.dot(cross, lags, preferred_element_type=jnp.float32).astype(jnp.bfloat16)
    return stacked.reshape(1, TILE, TILE, LAGS)


def solution(mesh):
    placed = (P(None, ("groups", "tiles"), None), P(), P(None, ("groups", "tiles")), P())
    return jax.shard_map(
        local,
        mesh=mesh,
        in_specs=placed,
        out_specs=P(("groups", "tiles"), None, None, None),
        check_vma=False,
    )
```

profile of v0, /device:TPU:0, one launch (start us, length us, event | category | flops | bytes accessed | tf_op | source)
XLA Modules:
  0.0 251.8 jit_solution(16928799047254272326)
XLA Ops:
  6.5 0.0 copy-start
  6.5 0.0 all-gather.2.cloned.1.call-start
  6.5 0.8 slice.33
  7.3 0.1 rev.3
  7.4 0.7 concatenate.26
  8.2 3.9 %tile.4 = f32[512,4160]{1,0:T(8,128)} broadcast(f32[4160]{0:T(1024)S(1)} %concatenate.26), dimensions={1} | broadcast | bytes 8536320 | tf_op jit(solution)/shard_map/tile | solution.py:19
  12.0 10.0 %tile.10 = f32[2129920]{0:T(1024)} reshape(f32[512,4160]{1,0:T(8,128)} %tile.4) | data formatting | bytes 17039360 | tf_op jit(solution)/shard_map/tile | solution.py:19
  22.0 7.8 %slice.42 = f32[2127872]{0:T(1024)} slice(f32[2129920]{0:T(1024)} %tile.10), slice={[0:2127872]} | slice | bytes 17022976 | tf_op jit(solution)/shard_map/slice | solution.py:19
  29.8 14.4 %reshape.66 = f32[512,4156]{1,0:T(8,128)} reshape(f32[2127872]{0:T(1024)} %slice.42) | data formatting | bytes 17022976 | tf_op jit(solution)/shard_map/reshape | solution.py:19
  44.1 0.0 copy-done
  44.2 0.0 copy-start.2
  44.2 0.0 copy-start.3
  44.2 4.8 %fusion.70 = (f32[16,512]{1,0:T(8,128)S(1)}, f32[16,8,512]{2,0,1:T(8,128)S(1)}) fusion(bf16[16,8,2048]{2,1,0:T(8,128)(2,1)S(1)} %copy-done, f32[512,4156]{1,0:T(8,128)} %reshape.66), kind=kOutput, calls=%fused_computation.98 | convolution fusion | flops 1610670080 | bytes 5013504 | tf_op jit(solution)/shard_map/wcm,nm->wcn/dot_general | solution.py:25
  49.0 62.9 %psum.7 = f32[16,512]{1,0:T(8,128)S(1)} all-reduce(f32[16,512]{1,0:T(8,128)S(1)} %get-tuple-element.15), channel_id=1, replica_groups=mesh['groups'=2,'tiles'=16] {'tiles'}, use_global_device_ids=true, to_apply=%region_1.0 | all-reduce | flops 8192 | bytes 65536 | tf_op jit(solution)/shard_map/psum | solution.py:74
  112.0 2.4 fusion.25
  114.4 2.5 fusion.46
  116.9 0.0 copy-done.2
  116.9 0.1 copy.19
  117.0 0.1 multiply_convert_fusion.1
  117.1 0.7 pad_maximum_fusion
  117.7 0.0 all-gather.2.cloned.1.call-update
  117.8 0.0 copy-done.3
  117.8 0.1 constant_dynamic-slice_fusion
  117.9 0.6 fusion.69
  119.8 36.6 %all-gather.2.cloned.1.call-done = bf16[16,128,512]{2,1,0:T(8,128)(2,1)} async-done(((bf16[16,8,512]{2,1,0:T(8,128)(2,1)}), bf16[16,128,512]{2,1,0:T(8,128)(2,1)}) %all-gather.2.cloned.1.call-update) | async-done | bytes 2097168 | tf_op jit(solution)/shard_map/all_gather | solution.py:81
  156.4 2.4 convert_bitcast_fusion
  158.8 2.4 convert_bitcast_fusion.1
  161.2 0.3 fusion.67
  161.5 8.1 %fusion.13 = f32[256,128,128]{2,1,0:T(8,128)} fusion(bf16[16,128,256]{1,2,0:T(8,128)(2,1)S(1)} %get-tuple-element.19, bf16[16,128,256]{1,2,0:T(8,128)(2,1)S(1)} %get-tuple-element.5), kind=kOutput, calls=%fused_computation.22 | convolution fusion | flops 134217728 | bytes 18874368 | tf_op jit(solution)/shard_map/wif,wjf->ijf/dot_general | solution.py:49
  169.6 8.1 %fusion.9 = f32[256,128,128]{2,1,0:T(8,128)} fusion(bf16[16,128,256]{1,2,0:T(8,128)(2,1)S(1)} %get-tuple-element.6, bf16[16,128,256]{1,2,0:T(8,128)(2,1)S(1)} %get-tuple-element.19), kind=kOutput, calls=%fused_computation.18 | convolution fusion | flops 134217728 | bytes 18874368 | tf_op jit(solution)/shard_map/wif,wjf->ijf/dot_general | solution.py:53
  177.6 12.9 %fusion.3 = bf16[128,128,256]{0,1,2:T(8,128)(2,1)} fusion(f32[256,128,128]{2,1,0:T(8,128)} %fusion.13, bf16[16,128,256]{1,2,0:T(8,128)(2,1)S(1)} %get-tuple-element.20, bf16[16,128,256]{1,2,0:T(8,128)(2,1)S(1)} %get-tuple-element.6), kind=kOutput, calls=%fused_computation.6 | convolution fusion | flops 142606336 | bytes 27262976 | tf_op jit(solution)/shard_map/wif,wjf->ijf/dot_general | solution.py:50
  190.5 13.5 %copy.25 = bf16[128,128,256]{2,1,0:T(8,128)(2,1)} copy(bf16[128,128,256]{0,1,2:T(8,128)(2,1)} %fusion.3) | data formatting | bytes 16777216 | tf_op jit(solution)/shard_map/add | solution.py:50
  204.0 12.9 %fusion.4 = bf16[128,128,256]{0,1,2:T(8,128)(2,1)} fusion(f32[256,128,128]{2,1,0:T(8,128)} %fusion.9, bf16[16,128,256]{1,2,0:T(8,128)(2,1)S(1)} %get-tuple-element.20, bf16[16,128,256]{1,2,0:T(8,128)(2,1)S(1)} %get-tuple-element.5), kind=kOutput, calls=%fused_computation.7 | convolution fusion | flops 142606336 | bytes 27262976 | tf_op jit(solution)/shard_map/wif,wjf->ijf/dot_general | solution.py:54
  216.9 13.5 %copy.30 = bf16[128,128,256]{2,1,0:T(8,128)(2,1)} copy(bf16[128,128,256]{0,1,2:T(8,128)(2,1)} %fusion.4) | data formatting | bytes 16777216 | tf_op jit(solution)/shard_map/sub | solution.py:54
  230.4 0.0 copy-start.1
  230.4 14.5 %convolution_convert_fusion = bf16[16384,256]{1,0:T(8,128)(2,1)} fusion(bf16[16384,256]{1,0:T(8,128)(2,1)} %bitcast.40, bf16[16384,256]{1,0:T(8,128)(2,1)} %bitcast.39, f32[512]{0:T(512)S(1)} %get-tuple-element.12, s32[256]{0:T(256)S(1)} %iota_add_fusion, s32[512]{0:T(512)S(1)} %pad_add_fusion, f32[512]{0:T(512)S(1)} %get-tuple-element.11, ...), kind=kOutput, calls=%fused_computation | convolution fusion | flops 4335075328 | bytes 25173504 | tf_op jit(solution)/shard_map/dot_general | solution.py:93
  245.0 0.0 copy-done.1
  (12 shorter events, 0.1 us)
Async XLA Ops:
  6.5 37.6 %copy-start = (bf16[16,8,2048]{2,1,0:T(8,128)(2,1)S(1)}, bf16[16,8,2048]{2,1,0:T(8,128)(2,1)}, u32[]{:S(2)}) copy-start(bf16[16,8,2048]{2,1,0:T(8,128)(2,1)} %param.4) | copy-start | bytes 1572868
  6.5 149.9 %all-gather.2.cloned.1.call-start = ((), (), s32[]{:S(2)}) async-start(), calls=%async_computation | async-start | bytes 2228224 | tf_op jit(solution)/shard_map/all_gather | solution.py:81
  44.2 72.7 %copy-start.2 = (s32[16,8]{0,1:T(8,128)S(1)}, s32[16,8]{0,1:T(8,128)}, u32[]{:S(2)}) copy-start(s32[16,8]{0,1:T(8,128)} %param.6) | copy-start | bytes 1540
  44.2 73.6 %copy-start.3 = (s32[16,2]{0,1:T(2,128)S(1)}, s32[16,2]{0,1:T(2,128)}, u32[]{:S(2)}) copy-start(s32[16,2]{0,1:T(2,128)} %param.7) | copy-start | bytes 388
  230.4 14.5 %copy-start.1 = (bf16[16,8,2048]{2,1,0:T(8,128)(2,1)S(1)}, bf16[16,8,2048]{2,1,0:T(8,128)(2,1)}, u32[]{:S(2)}) copy-start(bf16[16,8,2048]{2,1,0:T(8,128)(2,1)} %param.4) | copy-start | bytes 1572868
Sparse Core Ops, SparseCore 0:
  117.9 38.4 all-gather.1
where the time goes:
time: 253 us; the launch traced here: 252 us
  matrix products  71 us (28%)
  local copies, waits for them, and re-layouts  65.6 us (26%)
  blocking collectives  62.9 us (25%)
  waiting for transfers between devices  36.6 us (14%)
  between operations  14.8 us (6%)
    psum x1, blocking collectives, local(): channel_sum = lax.psum(jnp.sum(filtered, 1), 'tiles')  62.9 us
    all_gather x1, waiting for transfers between devices, local(): piece = lax.all_gather(whitened, 'tiles', axis=1, tiled=True)  36.6 us
    dot_general x1, matrix products, local(): jnp.dot(cross, lags, preferred_element_type=jnp.float32)  14.5 us
    reshape x1, local copies, waits for them, and re-layouts, filter_band(): jnp.tile(pattern, SEG)[:SEG * (period - DEC)].reshape(SEG, period - DEC)  14.4 us
    another operation x2, local copies, waits for them, and re-layouts, filter_band(): jnp.tile(pattern, SEG)[:SEG * (period - DEC)].reshape(SEG, period - DEC)  13.8 us
    sub x1, local copies, waits for them, and re-layouts, cross_tile(): cross_im - jnp.einsum('wif,wjf->ijf', row_im, col_re, preferred_element_t...  13.5 us
    add x1, local copies, waits for them, and re-layouts, cross_tile(): cross_re + jnp.einsum('wif,wjf->ijf', row_im, col_im, preferred_element_t...  13.5 us
    dot_general x1, matrix products, cross_tile(): jnp.einsum('wif,wjf->ijf', row_im, col_re, preferred_element_type=jnp.flo...  12.9 us
  transfers between devices with their start and end apart: 1, of which 1 were waited for; matrix products, arithmetic and copies ran while one was open for 0% of the time, Pallas kernels for 0%

commit v1 on v0

--- a/solution.py
+++ b/solution.py
@@ -78,7 +78,14 @@
     row_base = entry[0] * TILE
     col_base = entry[1] * TILE
     offsets = jnp.arange(TILE, dtype=jnp.int32)
-    piece = lax.all_gather(whitened, "tiles", axis=1, tiled=True)
+    ring = [whitened]
+    for hop in range(15):
+        ring.append(lax.ppermute(ring[-1], "tiles", [(dev, (dev + 1) % 16) for dev in range(16)]))
+    piece = jnp.roll(
+        jnp.concatenate(ring[::-1], axis=1),
+        (lax.axis_index("tiles") + 1) * ring[0].shape[1],
+        axis=1,
+    )
     places = jnp.arange(piece.shape[1], dtype=jnp.int32)
     pick_rows = (places[None, :] == row_base + offsets[:, None]).astype(jnp.bfloat16)
     pick_cols = (places[None, :] == col_base + offsets[:, None]).astype(jnp.bfloat16)

time: 253 us -> 304 us (1.20)
  waiting for transfers between devices: 36.6 us -> 104 us
  between operations: 14.8 us -> 1.7 us
  matrix products: 71 us -> 67.9 us
    ppermute x0 -> x15, waiting for transfers between devices: none -> 104 us  [local(): lax.ppermute(ring[-1], 'tiles', [(dev, (dev + 1) % 16) for dev in range(1...]
    all_gather x1 -> x0, waiting for transfers between devices: 36.6 us -> none  [local(): piece = lax.all_gather(whitened, 'tiles', axis=1, tiled=True)]
  transfers between devices with their start and end apart: 1 -> 15, of which waited for: 1 -> 15; matrix products, arithmetic and copies ran while one was open for 0% -> 0% of each run, Pallas kernels for 0% -> 0%
where the time goes in v1:
time: 304 us; the launch traced here: 303 us
  waiting for transfers between devices  104 us (34%)
  matrix products  67.9 us (22%)
  local copies, waits for them, and re-layouts  65.9 us (22%)
  blocking collectives  62.9 us (21%)
    ppermute x15, waiting for transfers between devices, local(): lax.ppermute(ring[-1], 'tiles', [(dev, (dev + 1) % 16) for dev in range(1...  104 us
    psum x1, blocking collectives, local(): channel_sum = lax.psum(jnp.sum(filtered, 1), 'tiles')  62.9 us
    dot_general x1, matrix products, local(): jnp.dot(cross, lags, preferred_element_type=jnp.float32)  14.5 us
    reshape x1, local copies, waits for them, and re-layouts, filter_band(): jnp.tile(pattern, SEG)[:SEG * (period - DEC)].reshape(SEG, period - DEC)  14.4 us
    another operation x2, local copies, waits for them, and re-layouts, filter_band(): jnp.tile(pattern, SEG)[:SEG * (period - DEC)].reshape(SEG, period - DEC)  13.8 us
    sub x1, local copies, waits for them, and re-layouts, cross_tile(): cross_im - jnp.einsum('wif,wjf->ijf', row_im, col_re, preferred_element_t...  13.5 us
    add x1, local copies, waits for them, and re-layouts, cross_tile(): cross_re + jnp.einsum('wif,wjf->ijf', row_im, col_im, preferred_element_t...  13.5 us
    dot_general x1, matrix products, cross_tile(): jnp.einsum('wif,wjf->ijf', row_im, col_re, preferred_element_type=jnp.flo...  12.9 us
  transfers between devices with their start and end apart: 15, of which 15 were waited for; matrix products, arithmetic and copies ran while one was open for 0% of the time, Pallas kernels for 0%

profile of v1, /device:TPU:0, one launch (start us, length us, event | category | flops | bytes accessed | tf_op | source)
XLA Modules:
  0.0 303.2 jit_solution(15996956427724556452)
XLA Ops:
  0.0 0.8 slice.33
  0.8 0.1 rev.3
  0.9 0.7 concatenate.32
  1.6 3.9 %tile.4 = f32[512,4160]{1,0:T(8,128)} broadcast(f32[4160]{0:T(1024)S(1)} %concatenate.32), dimensions={1} | broadcast | bytes 8536320 | tf_op jit(solution)/shard_map/tile | solution.py:19
  5.5 9.9 %tile.10 = f32[2129920]{0:T(1024)} reshape(f32[512,4160]{1,0:T(8,128)} %tile.4) | data formatting | bytes 17039360 | tf_op jit(solution)/shard_map/tile | solution.py:19
  15.5 7.8 %slice.42 = f32[2127872]{0:T(1024)} slice(f32[2129920]{0:T(1024)} %tile.10), slice={[0:2127872]} | slice | bytes 17022976 | tf_op jit(solution)/shard_map/slice | solution.py:19
  23.3 14.4 %reshape.66 = f32[512,4156]{1,0:T(8,128)} reshape(f32[2127872]{0:T(1024)} %slice.42) | data formatting | bytes 17022976 | tf_op jit(solution)/shard_map/reshape | solution.py:19
  37.7 4.8 %fusion.74 = (f32[16,512]{1,0:T(8,128)S(1)}, f32[16,8,512]{2,0,1:T(8,128)S(1)}) fusion(bf16[16,8,2048]{2,1,0:T(8,128)(2,1)S(1)} %copy-done, f32[512,4156]{1,0:T(8,128)} %reshape.66), kind=kOutput, calls=%fused_computation.134 | convolution fusion | flops 1610670080 | bytes 5013504 | tf_op jit(solution)/shard_map/wcm,nm->wcn/dot_general | solution.py:25
  42.5 0.0 copy-start.3
  42.5 62.9 %psum.7 = f32[16,512]{1,0:T(8,128)S(1)} all-reduce(f32[16,512]{1,0:T(8,128)S(1)} %get-tuple-element.15), channel_id=1, replica_groups=mesh['groups'=2,'tiles'=16] {'tiles'}, use_global_device_ids=true, to_apply=%region_1.0 | all-reduce | flops 8192 | bytes 65536 | tf_op jit(solution)/shard_map/psum | solution.py:74
  105.5 2.4 fusion.27
  107.9 2.5 fusion.48
  110.4 0.1 copy.21
  110.5 0.1 multiply_convert_fusion.1
  110.6 0.2 collective-permute-start
  110.9 7.1 %collective-permute-done = bf16[16,8,512]{2,1,0:T(8,128)(2,1)S(1)} collective-permute-done((bf16[16,8,512]{2,1,0:T(8,128)(2,1)S(1)}, bf16[16,8,512]{2,1,0:T(8,128)(2,1)S(1)}, u32[]{:S(2)}, u32[]{:S(2)}) %collective-permute-start) | collective-permute-done | bytes 131104 | tf_op jit(solution)/shard_map/ppermute | solution.py:83
  117.9 7.1 %collective-permute-done.1 = bf16[16,8,512]{2,1,0:T(8,128)(2,1)S(1)} collective-permute-done((bf16[16,8,512]{2,1,0:T(8,128)(2,1)S(1)}, bf16[16,8,512]{2,1,0:T(8,128)(2,1)S(1)}, u32[]{:S(2)}, u32[]{:S(2)}) %collective-permute-start.1) | collective-permute-done | bytes 131104 | tf_op jit(solution)/shard_map/ppermute | solution.py:83
  125.0 7.1 %collective-permute-done.2 = bf16[16,8,512]{2,1,0:T(8,128)(2,1)S(1)} collective-permute-done((bf16[16,8,512]{2,1,0:T(8,128)(2,1)S(1)}, bf16[16,8,512]{2,1,0:T(8,128)(2,1)S(1)}, u32[]{:S(2)}, u32[]{:S(2)}) %collective-permute-start.2) | collective-permute-done | bytes 131104 | tf_op jit(solution)/shard_map/ppermute | solution.py:83
  132.1 0.0 collective-permute-start.3
  132.1 7.1 %collective-permute-done.3 = bf16[16,8,512]{2,1,0:T(8,128)(2,1)S(1)} collective-permute-done((bf16[16,8,512]{2,1,0:T(8,128)(2,1)S(1)}, bf16[16,8,512]{2,1,0:T(8,128)(2,1)S(1)}, u32[]{:S(2)}, u32[]{:S(2)}) %collective-permute-start.3) | collective-permute-done | bytes 131104 | tf_op jit(solution)/shard_map/ppermute | solution.py:83
  139.2 0.0 collective-permute-start.4
  139.2 7.1 %collective-permute-done.4 = bf16[16,8,512]{2,1,0:T(8,128)(2,1)S(1)} collective-permute-done((bf16[16,8,512]{2,1,0:T(8,128)(2,1)S(1)}, bf16[16,8,512]{2,1,0:T(8,128)(2,1)S(1)}, u32[]{:S(2)}, u32[]{:S(2)}) %collective-permute-start.4) | collective-permute-done | bytes 131104 | tf_op jit(solution)/shard_map/ppermute | solution.py:83
  146.3 7.1 %collective-permute-done.5 = bf16[16,8,512]{2,1,0:T(8,128)(2,1)S(1)} collective-permute-done((bf16[16,8,512]{2,1,0:T(8,128)(2,1)S(1)}, bf16[16,8,512]{2,1,0:T(8,128)(2,1)S(1)}, u32[]{:S(2)}, u32[]{:S(2)}) %collective-permute-start.5) | collective-permute-done | bytes 131104 | tf_op jit(solution)/shard_map/ppermute | solution.py:83
  153.4 0.0 collective-permute-start.6
  153.4 7.1 %collective-permute-done.6 = bf16[16,8,512]{2,1,0:T(8,128)(2,1)S(1)} collective-permute-done((bf16[16,8,512]{2,1,0:T(8,128)(2,1)S(1)}, bf16[16,8,512]{2,1,0:T(8,128)(2,1)S(1)}, u32[]{:S(2)}, u32[]{:S(2)}) %collective-permute-start.6) | collective-permute-done | bytes 131104 | tf_op jit(solution)/shard_map/ppermute | solution.py:83
  160.5 0.0 collective-permute-start.7
  160.5 7.1 %collective-permute-done.7 = bf16[16,8,512]{2,1,0:T(8,128)(2,1)S(1)} collective-permute-done((bf16[16,8,512]{2,1,0:T(8,128)(2,1)S(1)}, bf16[16,8,512]{2,1,0:T(8,128)(2,1)S(1)}, u32[]{:S(2)}, u32[]{:S(2)}) %collective-permute-start.7) | collective-permute-done | bytes 131104 | tf_op jit(solution)/shard_map/ppermute | solution.py:83
  167.6 7.1 %collective-permute-done.8 = bf16[16,8,512]{2,1,0:T(8,128)(2,1)S(1)} collective-permute-done((bf16[16,8,512]{2,1,0:T(8,128)(2,1)S(1)}, bf16[16,8,512]{2,1,0:T(8,128)(2,1)S(1)}, u32[]{:S(2)}, u32[]{:S(2)}) %collective-permute-start.8) | collective-permute-done | bytes 131104 | tf_op jit(solution)/shard_map/ppermute | solution.py:83
  174.7 0.0 collective-permute-start.9
  174.7 7.1 %collective-permute-done.9 = bf16[16,8,512]{2,1,0:T(8,128)(2,1)S(1)} collective-permute-done((bf16[16,8,512]{2,1,0:T(8,128)(2,1)S(1)}, bf16[16,8,512]{2,1,0:T(8,128)(2,1)S(1)}, u32[]{:S(2)}, u32[]{:S(2)}) %collective-permute-start.9) | collective-permute-done | bytes 131104 | tf_op jit(solution)/shard_map/ppermute | solution.py:83
  181.7 0.0 collective-permute-start.10
  181.8 7.1 %collective-permute-done.10 = bf16[16,8,512]{2,1,0:T(8,128)(2,1)S(1)} collective-permute-done((bf16[16,8,512]{2,1,0:T(8,128)(2,1)S(1)}, bf16[16,8,512]{2,1,0:T(8,128)(2,1)S(1)}, u32[]{:S(2)}, u32[]{:S(2)}) %collective-permute-start.10) | collective-permute-done | bytes 131104 | tf_op jit(solution)/shard_map/ppermute | solution.py:83
  188.8 0.1 constant_dynamic-slice_fusion
  188.9 0.5 fusion.73
  189.5 6.5 %collective-permute-done.11 = bf16[16,8,512]{2,1,0:T(8,128)(2,1)S(1)} collective-permute-done((bf16[16,8,512]{2,1,0:T(8,128)(2,1)S(1)}, bf16[16,8,512]{2,1,0:T(8,128)(2,1)S(1)}, u32[]{:S(2)}, u32[]{:S(2)}) %collective-permute-start.11) | collective-permute-done | bytes 131104 | tf_op jit(solution)/shard_map/ppermute | solution.py:83
  196.6 6.4 %collective-permute-done.12 = bf16[16,8,512]{2,1,0:T(8,128)(2,1)S(1)} collective-permute-done((bf16[16,8,512]{2,1,0:T(8,128)(2,1)S(1)}, bf16[16,8,512]{2,1,0:T(8,128)(2,1)S(1)}, u32[]{:S(2)}, u32[]{:S(2)}) %collective-permute-start.12) | collective-permute-done | bytes 131104 | tf_op jit(solution)/shard_map/ppermute | solution.py:83
  203.7 6.4 %collective-permute-done.13 = bf16[16,8,512]{2,1,0:T(8,128)(2,1)S(1)} collective-permute-done((bf16[16,8,512]{2,1,0:T(8,128)(2,1)S(1)}, bf16[16,8,512]{2,1,0:T(8,128)(2,1)S(1)}, u32[]{:S(2)}, u32[]{:S(2)}) %collective-permute-start.13) | collective-permute-done | bytes 131104 | tf_op jit(solution)/shard_map/ppermute | solution.py:83
  210.1 7.1 %collective-permute-done.14 = bf16[16,8,512]{2,1,0:T(8,128)(2,1)S(1)} collective-permute-done((bf16[16,8,512]{2,1,0:T(8,128)(2,1)S(1)}, bf16[16,8,512]{2,1,0:T(8,128)(2,1)S(1)}, u32[]{:S(2)}, u32[]{:S(2)}) %collective-permute-start.14) | collective-permute-done | bytes 131104 | tf_op jit(solution)/shard_map/ppermute | solution.py:83
  217.8 0.8 convert_bitcast_fusion
  218.6 0.8 convert_bitcast_fusion.1
  219.4 0.3 fusion.71
  219.7 8.1 %fusion.15 = f32[256,128,128]{2,1,0:T(8,128)} fusion(bf16[16,128,256]{1,2,0:T(8,128)(2,1)S(1)} %get-tuple-element.19, bf16[16,128,256]{1,2,0:T(8,128)(2,1)S(1)} %get-tuple-element.5), kind=kOutput, calls=%fused_computation.24 | convolution fusion | flops 134217728 | bytes 18874368 | tf_op jit(solution)/shard_map/wif,wjf->ijf/dot_general | solution.py:49
  227.8 8.1 %fusion.11 = f32[256,128,128]{2,1,0:T(8,128)} fusion(bf16[16,128,256]{1,2,0:T(8,128)(2,1)S(1)} %get-tuple-element.6, bf16[16,128,256]{1,2,0:T(8,128)(2,1)S(1)} %get-tuple-element.19), kind=kOutput, calls=%fused_computation.20 | convolution fusion | flops 134217728 | bytes 18874368 | tf_op jit(solution)/shard_map/wif,wjf->ijf/dot_general | solution.py:53
  235.9 12.9 %fusion.3 = bf16[128,128,256]{0,1,2:T(8,128)(2,1)} fusion(f32[256,128,128]{2,1,0:T(8,128)} %fusion.15, bf16[16,128,256]{1,2,0:T(8,128)(2,1)S(1)} %get-tuple-element.20, bf16[16,128,256]{1,2,0:T(8,128)(2,1)S(1)} %get-tuple-element.6), kind=kOutput, calls=%fused_computation.6 | convolution fusion | flops 142606336 | bytes 27262976 | tf_op jit(solution)/shard_map/wif,wjf->ijf/dot_general | solution.py:50
  248.8 13.5 %copy.29 = bf16[128,128,256]{2,1,0:T(8,128)(2,1)} copy(bf16[128,128,256]{0,1,2:T(8,128)(2,1)} %fusion.3) | data formatting | bytes 16777216 | tf_op jit(solution)/shard_map/add | solution.py:50
  262.3 12.9 %fusion.4 = bf16[128,128,256]{0,1,2:T(8,128)(2,1)} fusion(f32[256,128,128]{2,1,0:T(8,128)} %fusion.11, bf16[16,128,256]{1,2,0:T(8,128)(2,1)S(1)} %get-tuple-element.20, bf16[16,128,256]{1,2,0:T(8,128)(2,1)S(1)} %get-tuple-element.5), kind=kOutput, calls=%fused_computation.7 | convolution fusion | flops 142606336 | bytes 27262976 | tf_op jit(solution)/shard_map/wif,wjf->ijf/dot_general | solution.py:54
  275.2 13.5 %copy.34 = bf16[128,128,256]{2,1,0:T(8,128)(2,1)} copy(bf16[128,128,256]{0,1,2:T(8,128)(2,1)} %fusion.4) | data formatting | bytes 16777216 | tf_op jit(solution)/shard_map/sub | solution.py:54
  288.7 14.5 %convolution_convert_fusion = bf16[16384,256]{1,0:T(8,128)(2,1)} fusion(bf16[16384,256]{1,0:T(8,128)(2,1)} %bitcast.38, bf16[16384,256]{1,0:T(8,128)(2,1)} %bitcast.37, f32[512]{0:T(512)S(1)} %get-tuple-element.12, s32[256]{0:T(256)S(1)} %iota_add_fusion, s32[512]{0:T(512)S(1)} %pad_add_fusion, f32[512]{0:T(512)S(1)} %get-tuple-element.11, ...), kind=kOutput, calls=%fused_computation | convolution fusion | flops 4335075328 | bytes 25173504 | tf_op jit(solution)/shard_map/dot_general | solution.py:100
  (60 shorter events, 0.5 us)
Async XLA Ops:
  0.0 37.7 %copy-start = (bf16[16,8,2048]{2,1,0:T(8,128)(2,1)S(1)}, bf16[16,8,2048]{2,1,0:T(8,128)(2,1)}, u32[]{:S(2)}) copy-start(bf16[16,8,2048]{2,1,0:T(8,128)(2,1)} %param.4) | copy-start | bytes 1572868
  37.7 72.7 %copy-start.2 = (s32[16,8]{0,1:T(8,128)S(1)}, s32[16,8]{0,1:T(8,128)}, u32[]{:S(2)}) copy-start(s32[16,8]{0,1:T(8,128)} %param.6) | copy-start | bytes 1540
  42.5 146.3 %copy-start.3 = (s32[16,2]{0,1:T(2,128)S(1)}, s32[16,2]{0,1:T(2,128)}, u32[]{:S(2)}) copy-start(s32[16,2]{0,1:T(2,128)} %param.7) | copy-start | bytes 388
  110.6 7.3 %collective-permute-start = (bf16[16,8,512]{2,1,0:T(8,128)(2,1)S(1)}, bf16[16,8,512]{2,1,0:T(8,128)(2,1)S(1)}, u32[]{:S(2)}, u32[]{:S(2)}) collective-permute-start(bf16[16,8,512]{2,1,0:T(8,128)(2,1)S(1)} %pad_maximum_fusion), channel_id=1, source_target_pairs={{0,1},{1,2},{2,3},{3,4},{4,5},{5,6},{6,7},{7,8},{8,9},{9,10},{10,1... | collective-permute-start | bytes 393224 | tf_op jit(solution)/shard_map/ppermute | solution.py:83
  117.9 7.1 %collective-permute-start.1 = (bf16[16,8,512]{2,1,0:T(8,128)(2,1)S(1)}, bf16[16,8,512]{2,1,0:T(8,128)(2,1)S(1)}, u32[]{:S(2)}, u32[]{:S(2)}) collective-permute-start(bf16[16,8,512]{2,1,0:T(8,128)(2,1)S(1)} %collective-permute-done), channel_id=1, source_target_pairs={{0,1},{1,2},{2,3},{3,4},{4,5},{5,6},{6,7},{7,8},{8,9},{9,10},{10,1... | collective-permute-start | bytes 393224 | tf_op jit(solution)/shard_map/ppermute | solution.py:83
  125.0 7.1 %collective-permute-start.2 = (bf16[16,8,512]{2,1,0:T(8,128)(2,1)S(1)}, bf16[16,8,512]{2,1,0:T(8,128)(2,1)S(1)}, u32[]{:S(2)}, u32[]{:S(2)}) collective-permute-start(bf16[16,8,512]{2,1,0:T(8,128)(2,1)S(1)} %collective-permute-done.1), channel_id=1, source_target_pairs={{0,1},{1,2},{2,3},{3,4},{4,5},{5,6},{6,7},{7,8},{8,9},{9,10},{10,1... | collective-permute-start | bytes 393224 | tf_op jit(solution)/shard_map/ppermute | solution.py:83
  132.1 7.1 %collective-permute-start.3 = (bf16[16,8,512]{2,1,0:T(8,128)(2,1)S(1)}, bf16[16,8,512]{2,1,0:T(8,128)(2,1)S(1)}, u32[]{:S(2)}, u32[]{:S(2)}) collective-permute-start(bf16[16,8,512]{2,1,0:T(8,128)(2,1)S(1)} %collective-permute-done.2), channel_id=1, source_target_pairs={{0,1},{1,2},{2,3},{3,4},{4,5},{5,6},{6,7},{7,8},{8,9},{9,10},{10,1... | collective-permute-start | bytes 393224 | tf_op jit(solution)/shard_map/ppermute | solution.py:83
  139.2 7.1 %collective-permute-start.4 = (bf16[16,8,512]{2,1,0:T(8,128)(2,1)S(1)}, bf16[16,8,512]{2,1,0:T(8,128)(2,1)S(1)}, u32[]{:S(2)}, u32[]{:S(2)}) collective-permute-start(bf16[16,8,512]{2,1,0:T(8,128)(2,1)S(1)} %collective-permute-done.3), channel_id=1, source_target_pairs={{0,1},{1,2},{2,3},{3,4},{4,5},{5,6},{6,7},{7,8},{8,9},{9,10},{10,1... | collective-permute-start | bytes 393224 | tf_op jit(solution)/shard_map/ppermute | solution.py:83
  146.3 7.1 %collective-permute-start.5 = (bf16[16,8,512]{2,1,0:T(8,128)(2,1)S(1)}, bf16[16,8,512]{2,1,0:T(8,128)(2,1)S(1)}, u32[]{:S(2)}, u32[]{:S(2)}) collective-permute-start(bf16[16,8,512]{2,1,0:T(8,128)(2,1)S(1)} %collective-permute-done.4), channel_id=1, source_target_pairs={{0,1},{1,2},{2,3},{3,4},{4,5},{5,6},{6,7},{7,8},{8,9},{9,10},{10,1... | collective-permute-start | bytes 393224 | tf_op jit(solution)/shard_map/ppermute | solution.py:83
  153.4 7.1 %collective-permute-start.6 = (bf16[16,8,512]{2,1,0:T(8,128)(2,1)S(1)}, bf16[16,8,512]{2,1,0:T(8,128)(2,1)S(1)}, u32[]{:S(2)}, u32[]{:S(2)}) collective-permute-start(bf16[16,8,512]{2,1,0:T(8,128)(2,1)S(1)} %collective-permute-done.5), channel_id=1, source_target_pairs={{0,1},{1,2},{2,3},{3,4},{4,5},{5,6},{6,7},{7,8},{8,9},{9,10},{10,1... | collective-permute-start | bytes 393224 | tf_op jit(solution)/shard_map/ppermute | solution.py:83
  160.5 7.1 %collective-permute-start.7 = (bf16[16,8,512]{2,1,0:T(8,128)(2,1)S(1)}, bf16[16,8,512]{2,1,0:T(8,128)(2,1)S(1)}, u32[]{:S(2)}, u32[]{:S(2)}) collective-permute-start(bf16[16,8,512]{2,1,0:T(8,128)(2,1)S(1)} %collective-permute-done.6), channel_id=1, source_target_pairs={{0,1},{1,2},{2,3},{3,4},{4,5},{5,6},{6,7},{7,8},{8,9},{9,10},{10,1... | collective-permute-start | bytes 393224 | tf_op jit(solution)/shard_map/ppermute | solution.py:83
  167.6 7.1 %collective-permute-start.8 = (bf16[16,8,512]{2,1,0:T(8,128)(2,1)S(1)}, bf16[16,8,512]{2,1,0:T(8,128)(2,1)S(1)}, u32[]{:S(2)}, u32[]{:S(2)}) collective-permute-start(bf16[16,8,512]{2,1,0:T(8,128)(2,1)S(1)} %collective-permute-done.7), channel_id=1, source_target_pairs={{0,1},{1,2},{2,3},{3,4},{4,5},{5,6},{6,7},{7,8},{8,9},{9,10},{10,1... | collective-permute-start | bytes 393224 | tf_op jit(solution)/shard_map/ppermute | solution.py:83
  174.7 7.1 %collective-permute-start.9 = (bf16[16,8,512]{2,1,0:T(8,128)(2,1)S(1)}, bf16[16,8,512]{2,1,0:T(8,128)(2,1)S(1)}, u32[]{:S(2)}, u32[]{:S(2)}) collective-permute-start(bf16[16,8,512]{2,1,0:T(8,128)(2,1)S(1)} %collective-permute-done.8), channel_id=1, source_target_pairs={{0,1},{1,2},{2,3},{3,4},{4,5},{5,6},{6,7},{7,8},{8,9},{9,10},{10,1... | collective-permute-start | bytes 393224 | tf_op jit(solution)/shard_map/ppermute | solution.py:83
  181.7 7.1 %collective-permute-start.10 = (bf16[16,8,512]{2,1,0:T(8,128)(2,1)S(1)}, bf16[16,8,512]{2,1,0:T(8,128)(2,1)S(1)}, u32[]{:S(2)}, u32[]{:S(2)}) collective-permute-start(bf16[16,8,512]{2,1,0:T(8,128)(2,1)S(1)} %collective-permute-done.9), channel_id=1, source_target_pairs={{0,1},{1,2},{2,3},{3,4},{4,5},{5,6},{6,7},{7,8},{8,9},{9,10},{10,1... | collective-permute-start | bytes 393224 | tf_op jit(solution)/shard_map/ppermute | solution.py:83
  188.8 7.1 %collective-permute-start.11 = (bf16[16,8,512]{2,1,0:T(8,128)(2,1)S(1)}, bf16[16,8,512]{2,1,0:T(8,128)(2,1)S(1)}, u32[]{:S(2)}, u32[]{:S(2)}) collective-permute-start(bf16[16,8,512]{2,1,0:T(8,128)(2,1)S(1)} %collective-permute-done.10), channel_id=1, source_target_pairs={{0,1},{1,2},{2,3},{3,4},{4,5},{5,6},{6,7},{7,8},{8,9},{9,10},{10,1... | collective-permute-start | bytes 393224 | tf_op jit(solution)/shard_map/ppermute | solution.py:83
  195.9 7.1 %collective-permute-start.12 = (bf16[16,8,512]{2,1,0:T(8,128)(2,1)S(1)}, bf16[16,8,512]{2,1,0:T(8,128)(2,1)S(1)}, u32[]{:S(2)}, u32[]{:S(2)}) collective-permute-start(bf16[16,8,512]{2,1,0:T(8,128)(2,1)S(1)} %collective-permute-done.11), channel_id=1, source_target_pairs={{0,1},{1,2},{2,3},{3,4},{4,5},{5,6},{6,7},{7,8},{8,9},{9,10},{10,1... | collective-permute-start | bytes 393224 | tf_op jit(solution)/shard_map/ppermute | solution.py:83
  203.0 7.1 %collective-permute-start.13 = (bf16[16,8,512]{2,1,0:T(8,128)(2,1)S(1)}, bf16[16,8,512]{2,1,0:T(8,128)(2,1)S(1)}, u32[]{:S(2)}, u32[]{:S(2)}) collective-permute-start(bf16[16,8,512]{2,1,0:T(8,128)(2,1)S(1)} %collective-permute-done.12), channel_id=1, source_target_pairs={{0,1},{1,2},{2,3},{3,4},{4,5},{5,6},{6,7},{7,8},{8,9},{9,10},{10,1... | collective-permute-start | bytes 393224 | tf_op jit(solution)/shard_map/ppermute | solution.py:83
  210.1 7.1 %collective-permute-start.14 = (bf16[16,8,512]{2,1,0:T(8,128)(2,1)S(1)}, bf16[16,8,512]{2,1,0:T(8,128)(2,1)S(1)}, u32[]{:S(2)}, u32[]{:S(2)}) collective-permute-start(bf16[16,8,512]{2,1,0:T(8,128)(2,1)S(1)} %collective-permute-done.13), channel_id=1, source_target_pairs={{0,1},{1,2},{2,3},{3,4},{4,5},{5,6},{6,7},{7,8},{8,9},{9,10},{10,1... | collective-permute-start | bytes 393224 | tf_op jit(solution)/shard_map/ppermute | solution.py:83
  288.7 14.5 %copy-start.1 = (bf16[16,8,2048]{2,1,0:T(8,128)(2,1)S(1)}, bf16[16,8,2048]{2,1,0:T(8,128)(2,1)}, u32[]{:S(2)}) copy-start(bf16[16,8,2048]{2,1,0:T(8,128)(2,1)} %param.4) | copy-start | bytes 1572868
